TPU v7x, 32 devices: a whole 2x2x4 slice. The times are simulated.
32 devices in a mesh: xy: 16 (over z, y, core), gz: 2 (over x).
Axes of the slice: x: 2, y: 2, z: 4, core: 2. Of those that a mesh axis runs over, the one named last changes fastest.
Arguments:
- hidden_features: bfloat16 [16, 16, 16, 512], P('gz', None, 'xy'), may hold values from -6 to 6
- scaling_factors_prenormal: float32 [512], replicated, may hold values from 0.1 to 1.9
- attention_input_matrices: bfloat16 [3, 512, 1536], P(None, 'xy'), may hold values from -1 to 1
- final_projection_matrices: bfloat16 [3, 512, 512], P(None, 'xy'), may hold values from -0.25 to 0.25
- score_scaling: float32 [3, 8], replicated, may hold values from 0 to 40
- filled_pillar_positions: int32 [16, 16], P('xy'), may hold values from 0 to 15, as said below
- filled_pillar_totals: int32 [16], P('xy'), may hold values from 4 to 16, as said below
Outputs:
- block_out: bfloat16 [16, 16, 16, 512], P('gz', None, 'xy')
Inputs may be any that keep to these rules, and one draw needn't show every extreme that they name: Row t of filled_pillar_positions is a permutation of 0 to 15; an entry c names the column x = c, y = t. `filled_pillar_totals`: some tile has all of its 16 columns occupied.
All inputs are finite; a program needn't handle non-finite values.
Results may differ from a plain program's by a relative error of at most 0.012.
Values may be sent and summed in bfloat16 or wider, within the bound.
No kernel may reach another device: no remote copies, remote signals or barrier semaphores. Data moves between devices by JAX's collectives and lax.ppermute only.
A program may use at most 64 MiB of HBM per device.

v0:
```python
import math
import jax
import jax.numpy as jnp
from jax import lax
from jax.sharding import PartitionSpec as P

EPSILON = 1e-06


def rms_scale(vector_rows):
    return vector_rows * lax.rsqrt(
        jnp.mean(vector_rows * vector_rows, axis=-1, keepdims=True) + EPSILON
    )


def project_qkv(tokens_in, w_project, attention_parts_number):
    projected = jnp.dot(tokens_in, w_project, preferred_element_type=jnp.float32)
    outer_shape = projected.shape[:-1]
    channels = w_project.shape[0]
    split_rows = projected.reshape(
        outer_shape + (3, attention_parts_number, channels // attention_parts_number)
    )
    queries = (
        rms_scale(split_rows[..., 0, :, :]).reshape(outer_shape + (channels,)).astype(jnp.bfloat16)
    )
    key_rows = (
        rms_scale(split_rows[..., 1, :, :]).reshape(outer_shape + (channels,)).astype(jnp.bfloat16)
    )
    values = split_rows[..., 2, :, :].reshape(outer_shape + (channels,)).astype(jnp.bfloat16)
    return (queries, key_rows, values)


def softmax_over_fibers(queries, key_rows, values, temper_row):
    attention_parts_number = temper_row.shape[0]
    outer_size, query_len, inner_size, channels = queries.shape
    key_len = key_rows.shape[1]
    head_dim = channels // attention_parts_number
    query_heads = queries.reshape(
        outer_size, query_len, inner_size, attention_parts_number, head_dim
    )
    key_heads = key_rows.reshape(outer_size, key_len, inner_size, attention_parts_number, head_dim)
    value_heads = values.reshape(outer_size, key_len, inner_size, attention_parts_number, head_dim)
    scores = jnp.einsum(
        "anbhd,ambhd->abhnm", query_heads, key_heads, preferred_element_type=jnp.float32
    )
    scores = scores * (temper_row / math.sqrt(head_dim))[None, None, :, None, None]
    weights = jax.nn.softmax(scores, axis=-1).astype(jnp.bfloat16)
    mixture = jnp.einsum(
        "abhnm,ambhd->anbhd", weights, value_heads, preferred_element_type=jnp.float32
    )
    return mixture.astype(jnp.bfloat16).reshape(outer_size, query_len, inner_size, channels)


def out_project(mixture, w_back):
    return jnp.dot(mixture, w_back, preferred_element_type=jnp.float32).astype(jnp.bfloat16)


def shards(
    hidden_features,
    scaling_factors_prenormal,
    attention_input_matrices,
    final_projection_matrices,
    score_scaling,
    filled_pillar_positions,
    filled_pillar_totals,
):
    full_qkv, full_out = (
        lax.all_gather(attention_input_matrices, "xy", axis=1, tiled=True),
        lax.all_gather(final_projection_matrices, "xy", axis=1, tiled=True),
    )
    attention_parts_number = score_scaling.shape[1]
    x_local, z_cells, y_rows, channels = hidden_features.shape
    normed = (rms_scale(hidden_features.astype(jnp.float32)) * scaling_factors_prenormal).astype(
        jnp.bfloat16
    )
    y_lines = normed.reshape(x_local * z_cells, y_rows, channels)
    local_query, local_keys, local_values = project_qkv(
        y_lines, full_qkv[1], attention_parts_number
    )
    query_along_y, keys_along_y, values_along_y = (
        lax.all_to_all(local_query, "xy", split_axis=0, concat_axis=1, tiled=True),
        lax.all_to_all(local_keys, "xy", split_axis=0, concat_axis=1, tiled=True),
        lax.all_to_all(local_values, "xy", split_axis=0, concat_axis=1, tiled=True),
    )
    y_mix = softmax_over_fibers(
        query_along_y[:, :, None, :],
        keys_along_y[:, :, None, :],
        values_along_y[:, :, None, :],
        score_scaling[1],
    )[:, :, 0, :]
    second_direction_answer = lax.all_to_all(
        out_project(y_mix, full_out[1]), "xy", split_axis=1, concat_axis=0, tiled=True
    ).reshape(hidden_features.shape)
    pieces = project_qkv(
        lax.all_to_all(normed, "gz", split_axis=1, concat_axis=0, tiled=True),
        full_qkv[0],
        attention_parts_number,
    )
    full_len, slab_part, items, _ = pieces[0].shape
    shaped = (1, full_len, slab_part * items, channels)
    x_mix = softmax_over_fibers(
        pieces[0].reshape(shaped),
        pieces[1].reshape(shaped),
        pieces[2].reshape(shaped),
        score_scaling[0],
    )
    result_rows = out_project(x_mix, full_out[0]).reshape(full_len, slab_part, items, channels)
    first_direction_answer = lax.all_to_all(
        result_rows, "gz", split_axis=0, concat_axis=1, tiled=True
    )
    cols_here = x_local * y_rows
    total_cols = filled_pillar_positions.shape[1]
    my_cols = lax.axis_index("gz") * cols_here + jnp.arange(cols_here, dtype=jnp.int32)
    live_rank = jnp.arange(total_cols, dtype=jnp.int32) < filled_pillar_totals[0]
    matches = filled_pillar_positions[0][None, :] == my_cols[:, None]
    live = jnp.any(jnp.logical_and(matches, live_rank[None, :]), axis=1)
    vertical_asking_terms, vertical_matching_terms, vertical_content_terms = project_qkv(
        normed, full_qkv[2], attention_parts_number
    )
    vertical_blended = softmax_over_fibers(
        vertical_asking_terms, vertical_matching_terms, vertical_content_terms, score_scaling[2]
    )
    z_full = out_project(vertical_blended, full_out[2])
    live_grid = live.reshape(x_local, 1, y_rows, 1)
    vertical_answer = jnp.where(live_grid, z_full, jnp.zeros_like(z_full))
    summed = (
        hidden_features.astype(jnp.float32)
        + first_direction_answer.astype(jnp.float32)
        + second_direction_answer.astype(jnp.float32)
    )
    summed = summed + vertical_answer.astype(jnp.float32)
    return summed.astype(jnp.bfloat16)


def solution(mesh):
    in_specs = (
        P("gz", None, "xy", None),
        P(),
        P(None, "xy", None),
        P(None, "xy", None),
        P(),
        P("xy", None),
        P("xy"),
    )
    out_specs = P("gz", None, "xy", None)
    return jax.shard_map(shards, mesh=mesh, in_specs=in_specs, out_specs=out_specs, check_vma=False)
```

profile of v0, /device:TPU:0, one launch (start us, length us, event | category | flops | bytes accessed | tf_op | source)
XLA Modules:
  0.0 148.3 jit_solution(13666185661406171766)
XLA Ops:
  6.5 0.7 all-gather.3.cloned.1.call-update
  7.3 1.0 fusion.23
  8.3 1.0 fusion.25
  9.3 0.7 copy.102
  10.0 4.2 %all-to-all-start = ((bf16[8,16,1,512]{3,0,2,1:T(8,128)(2,1)}), bf16[8,16,1,512]{3,0,2,1:T(8,128)(2,1)S(1)}, u32[]{:S(2)}, u32[]{:S(2)}) async-start(bf16[8,16,1,512]{3,0,2,1:T(8,128)(2,1)} %copy.102), calls=%async_computation | async-start | bytes 262144 | tf_op jit(solution)/shard_map/all_to_all | solution.py:95
  14.3 0.7 all-gather.5.cloned.1.call-update
  15.0 0.8 multiply_bitcast_fusion.2
  16.5 0.8 and_reduce_fusion
  17.3 1.5 %all-to-all-done = bf16[8,16,1,512]{3,0,2,1:T(8,128)(2,1)S(1)} async-done(((bf16[8,16,1,512]{3,0,2,1:T(8,128)(2,1)}), bf16[8,16,1,512]{3,0,2,1:T(8,128)(2,1)S(1)}, u32[]{:S(2)}, u32[]{:S(2)}) %all-to-all-start) | async-done | bytes 131104 | tf_op jit(solution)/shard_map/all_to_all | solution.py:95
  18.8 0.7 copy.103
  19.5 46.0 %all-gather.3.cloned.1.call-done = bf16[3,512,1536]{2,1,0:T(8,128)(2,1)} async-done(((bf16[3,32,1536]{2,1,0:T(8,128)(2,1)}), bf16[3,512,1536]{2,1,0:T(8,128)(2,1)}) %all-gather.3.cloned.1.call-update) | async-done | bytes 4718608 | tf_op jit(solution)/shard_map/all_gather | solution.py:68
  65.5 4.4 %slice_bitcast_fusion.2 = (bf16[1536,512]{0,1:T(8,128)(2,1)}, bf16[1536,512]{0,1:T(8,128)(2,1)S(1)}, bf16[1536,512]{0,1:T(8,128)(2,1)}) fusion(bf16[3,512,1536]{2,1,0:T(8,128)(2,1)} %all-gather.3.cloned.1.call-done), kind=kLoop, calls=%fused_computation.5 | loop fusion | bytes 9437184 | tf_op jit(solution)/shard_map/dot_general | solution.py:17
  69.9 1.7 %copy.104 = bf16[1536,512]{1,0:T(8,128)(2,1)S(1)} copy(bf16[1536,512]{0,1:T(8,128)(2,1)} %get-tuple-element.11) | data formatting | bytes 3145728 | tf_op jit(solution)/shard_map/dot_general | solution.py:17
  71.6 2.6 %copy.112 = bf16[1536,512]{1,0:T(8,128)(2,1)} copy(bf16[1536,512]{0,1:T(8,128)(2,1)} %get-tuple-element.13) | data formatting | bytes 3145728 | tf_op jit(solution)/shard_map/dot_general | solution.py:17
  74.3 2.0 %convolution_bitcast_fusion.2 = f32[128,1,3,8,64]{0,4,3,2,1:T(8,128)S(1)} fusion(bf16[128,512,1,1]{1,0,3,2:T(8,128)(2,1)S(1)} %bitcast.200, bf16[3,8,64,512]{3,2,1,0:T(8,128)(2,1)} %bitcast.199), kind=kOutput, calls=%fused_computation.8 | convolution fusion | flops 201326592 | bytes 2490368 | tf_op jit(solution)/shard_map/dot_general | solution.py:17
  76.3 0.9 copy-done
  77.3 0.5 broadcast.203
  77.8 1.2 reduce.26
  79.0 1.0 copy.180
  80.1 0.7 reshape.552
  80.8 3.5 %all-to-all-start.3 = ((bf16[16,2,2048]{2,1,0:T(2,128)(2,1)}), bf16[16,2,2048]{2,1,0:T(2,128)(2,1)S(1)}, u32[]{:S(2)}, u32[]{:S(2)}) async-start(bf16[16,2,2048]{2,1,0:T(2,128)(2,1)} %reshape.552), calls=%async_computation.3 | async-start | bytes 262144 | tf_op jit(solution)/shard_map/all_to_all | solution.py:81
  84.3 1.8 %convolution_bitcast_fusion.1 = f32[16,8,1,3,8,64]{5,1,4,3,0,2:T(8,128)S(1)} fusion(bf16[16,8,512,1,1]{2,1,4,3,0:T(8,128)(2,1)} %bitcast.207, bf16[3,8,64,512,1]{3,2,1,0,4:T(8,128)(2,1)S(1)} %bitcast.197), kind=kOutput, calls=%fused_computation.7 | convolution fusion | flops 201326592 | bytes 2490368 | tf_op jit(solution)/shard_map/dot_general | solution.py:17
  86.5 0.4 fusion.22
  86.9 0.8 fusion.60
  87.7 1.0 fusion.9
  88.7 0.6 reduce.25
  89.4 0.7 reshape.550
  90.1 0.7 copy.125
  90.8 0.9 convolution_bitcast_fusion
  91.8 0.4 all-to-all-done.3
  92.2 5.8 %all-to-all-start.4 = ((bf16[16,2,2048]{2,1,0:T(2,128)(2,1)}), bf16[16,2,2048]{2,1,0:T(2,128)(2,1)S(1)}, u32[]{:S(2)}, u32[]{:S(2)}) async-start(bf16[16,2,2048]{2,1,0:T(2,128)(2,1)} %reshape.550), calls=%async_computation.4 | async-start | bytes 262144 | tf_op jit(solution)/shard_map/all_to_all | solution.py:82
  98.3 1.0 slice.122
  99.6 0.6 reduce.27
  100.3 0.7 reshape.554
  101.0 5.2 %all-to-all-done.4 = bf16[16,2,2048]{2,1,0:T(2,128)(2,1)S(1)} async-done(((bf16[16,2,2048]{2,1,0:T(2,128)(2,1)}), bf16[16,2,2048]{2,1,0:T(2,128)(2,1)S(1)}, u32[]{:S(2)}, u32[]{:S(2)}) %all-to-all-start.4) | async-done | bytes 131104 | tf_op jit(solution)/shard_map/all_to_all | solution.py:82
  106.2 3.5 %all-to-all-start.2 = ((bf16[16,2,2048]{2,1,0:T(2,128)(2,1)}), bf16[16,2,2048]{2,1,0:T(2,128)(2,1)S(1)}, u32[]{:S(2)}, u32[]{:S(2)}) async-start(bf16[16,2,2048]{2,1,0:T(2,128)(2,1)} %reshape.554), calls=%async_computation.2 | async-start | bytes 262144 | tf_op jit(solution)/shard_map/all_to_all | solution.py:83
  109.8 2.0 %fusion.54 = (f32[8,8,16]{2,1,0:T(8,128)}, f32[8,8,16,16]{2,3,1,0:T(8,128)}) fusion(f32[8,16,1,3,8,64]{5,1,4,3,0,2:T(8,128)S(1)} %convolution_bitcast_fusion, f32[8]{0:T(128)S(1)} %get-tuple-element.19, f32[8,16,8]{1,2,0:T(8,128)S(1)} %get-tuple-element.27, f32[8,16,8]{1,2,0:T(8,128)S(1)} %get-tuple-element.28), kind=kOutput, calls=%fused_computation.99 | convolution fusion | flops 2408463 | bytes 1184256 | tf_op jit(solution)/shard_map/sub | solution.py:47
  112.4 5.2 %all-to-all-done.2 = bf16[16,2,2048]{2,1,0:T(2,128)(2,1)S(1)} async-done(((bf16[16,2,2048]{2,1,0:T(2,128)(2,1)}), bf16[16,2,2048]{2,1,0:T(2,128)(2,1)S(1)}, u32[]{:S(2)}, u32[]{:S(2)}) %all-to-all-start.2) | async-done | bytes 131104 | tf_op jit(solution)/shard_map/all_to_all | solution.py:83
  118.0 0.5 fusion.55
  119.1 1.3 convolution_convert_fusion.4
  120.4 0.7 copy.124
  121.2 3.6 %all-to-all-start.5 = ((bf16[8,16,512]{2,0,1:T(8,128)(2,1)}), bf16[8,16,512]{2,0,1:T(8,128)(2,1)S(1)}, u32[]{:S(2)}, u32[]{:S(2)}) async-start(bf16[8,16,512]{2,0,1:T(8,128)(2,1)} %copy.124), calls=%async_computation.5 | async-start | bytes 262144 | tf_op jit(solution)/shard_map/all_to_all | solution.py:91
  124.8 1.3 fusion.11
  126.4 0.9 fusion.12
  127.3 5.3 %all-to-all-done.5 = bf16[8,16,512]{2,0,1:T(8,128)(2,1)S(1)} async-done(((bf16[8,16,512]{2,0,1:T(8,128)(2,1)}), bf16[8,16,512]{2,0,1:T(8,128)(2,1)S(1)}, u32[]{:S(2)}, u32[]{:S(2)}) %all-to-all-start.5) | async-done | bytes 131104 | tf_op jit(solution)/shard_map/all_to_all | solution.py:91
  132.7 3.4 %all-to-all-start.1 = ((bf16[16,8,1,512]{3,1,2,0:T(8,128)(2,1)}), bf16[16,8,1,512]{3,1,2,0:T(8,128)(2,1)S(1)}, u32[]{:S(2)}, u32[]{:S(2)}) async-start(bf16[16,8,1,512]{3,1,2,0:T(8,128)(2,1)} %fusion.12), calls=%async_computation.1 | async-start | bytes 262144 | tf_op jit(solution)/shard_map/all_to_all | solution.py:108
  136.1 4.4 %all-to-all-done.1 = bf16[16,8,1,512]{3,1,2,0:T(8,128)(2,1)S(1)} async-done(((bf16[16,8,1,512]{3,1,2,0:T(8,128)(2,1)}), bf16[16,8,1,512]{3,1,2,0:T(8,128)(2,1)S(1)}, u32[]{:S(2)}, u32[]{:S(2)}) %all-to-all-start.1) | async-done | bytes 131104 | tf_op jit(solution)/shard_map/all_to_all | solution.py:108
  140.5 0.9 fusion.18
  (45 shorter events, 3.4 us)
Async XLA Ops:
  6.5 59.0 %all-gather.3.cloned.1.call-start = ((), (), s32[]{:S(2)}) async-start(), calls=%async_computation.6 | async-start | bytes 5013504 | tf_op jit(solution)/shard_map/all_gather | solution.py:68
  10.0 8.8 %all-to-all-start = ((bf16[8,16,1,512]{3,0,2,1:T(8,128)(2,1)}), bf16[8,16,1,512]{3,0,2,1:T(8,128)(2,1)S(1)}, u32[]{:S(2)}, u32[]{:S(2)}) async-start(bf16[8,16,1,512]{3,0,2,1:T(8,128)(2,1)} %copy.102), calls=%async_computation | async-start | bytes 262144 | tf_op jit(solution)/shard_map/all_to_all | solution.py:95
  14.3 104.9 %all-gather.5.cloned.1.call-start = ((), (), s32[]{:S(2)}) async-start(), calls=%async_computation.7 | async-start | bytes 1671168 | tf_op jit(solution)/shard_map/all_gather | solution.py:69
  76.2 0.9 copy-start
  80.8 11.4 %all-to-all-start.3 = ((bf16[16,2,2048]{2,1,0:T(2,128)(2,1)}), bf16[16,2,2048]{2,1,0:T(2,128)(2,1)S(1)}, u32[]{:S(2)}, u32[]{:S(2)}) async-start(bf16[16,2,2048]{2,1,0:T(2,128)(2,1)} %reshape.552), calls=%async_computation.3 | async-start | bytes 262144 | tf_op jit(solution)/shard_map/all_to_all | solution.py:81
  91.7 7.5 %copy-start.3 = (bf16[1,16,8,8,64]{4,1,3,2,0:T(8,128)(2,1)S(1)}, bf16[1,16,8,8,64]{4,1,3,2,0:T(8,128)(2,1)}, u32[]{:S(2)}) copy-start(bf16[1,16,8,8,64]{4,1,3,2,0:T(8,128)(2,1)} %fusion.9) | copy-start | bytes 393220
  92.2 14.1 %all-to-all-start.4 = ((bf16[16,2,2048]{2,1,0:T(2,128)(2,1)}), bf16[16,2,2048]{2,1,0:T(2,128)(2,1)S(1)}, u32[]{:S(2)}, u32[]{:S(2)}) async-start(bf16[16,2,2048]{2,1,0:T(2,128)(2,1)} %reshape.550), calls=%async_computation.4 | async-start | bytes 262144 | tf_op jit(solution)/shard_map/all_to_all | solution.py:82
  106.2 11.4 %all-to-all-start.2 = ((bf16[16,2,2048]{2,1,0:T(2,128)(2,1)}), bf16[16,2,2048]{2,1,0:T(2,128)(2,1)S(1)}, u32[]{:S(2)}, u32[]{:S(2)}) async-start(bf16[16,2,2048]{2,1,0:T(2,128)(2,1)} %reshape.554), calls=%async_computation.2 | async-start | bytes 262144 | tf_op jit(solution)/shard_map/all_to_all | solution.py:83
  118.8 6.0 %copy-start.4 = (f32[8,8,16]{2,1,0:T(8,128)S(1)}, f32[8,8,16]{2,1,0:T(8,128)}, u32[]{:S(2)}) copy-start(f32[8,8,16]{2,1,0:T(8,128)} %get-tuple-element.21) | copy-start | bytes 12292
  121.1 5.3 %copy-start.2 = (bf16[3,512,512]{2,1,0:T(8,128)(2,1)S(1)}, bf16[3,512,512]{2,1,0:T(8,128)(2,1)}, u32[]{:S(2)}) copy-start(bf16[3,512,512]{2,1,0:T(8,128)(2,1)} %all-gather.5.cloned.1.call-done) | copy-start | bytes 4718596
  121.2 11.5 %all-to-all-start.5 = ((bf16[8,16,512]{2,0,1:T(8,128)(2,1)}), bf16[8,16,512]{2,0,1:T(8,128)(2,1)S(1)}, u32[]{:S(2)}, u32[]{:S(2)}) async-start(bf16[8,16,512]{2,0,1:T(8,128)(2,1)} %copy.124), calls=%async_computation.5 | async-start | bytes 262144 | tf_op jit(solution)/shard_map/all_to_all | solution.py:91
  126.1 14.4 %copy-start.1 = (bf16[8,16,1,512]{3,1,2,0:T(8,128)(2,1)S(1)}, bf16[8,16,1,512]{3,1,2,0:T(8,128)(2,1)}, u32[]{:S(2)}) copy-start(bf16[8,16,1,512]{3,1,2,0:T(8,128)(2,1)} %param.7) | copy-start | bytes 393220
  132.7 7.8 %all-to-all-start.1 = ((bf16[16,8,1,512]{3,1,2,0:T(8,128)(2,1)}), bf16[16,8,1,512]{3,1,2,0:T(8,128)(2,1)S(1)}, u32[]{:S(2)}, u32[]{:S(2)}) async-start(bf16[16,8,1,512]{3,1,2,0:T(8,128)(2,1)} %fusion.12), calls=%async_computation.1 | async-start | bytes 262144 | tf_op jit(solution)/shard_map/all_to_all | solution.py:108
Sparse Core Ops, SparseCore 0:
  9.6 55.8 all-gather.2
  67.7 39.1 all-gather.4
where the time goes:
time: 149 us; the launch traced here: 148 us
  waiting for transfers between devices  69.6 us (47%)
  starting transfers between devices  24.1 us (16%)
  local copies, waits for them, and re-layouts  19.2 us (13%)
  between operations  14.4 us (10%)
  matrix products  13.7 us (9%)
  other arithmetic  7.31 us (5%)
    all_gather x1, waiting for transfers between devices, shards(): lax.all_gather(attention_input_matrices, 'xy', axis=1, tiled=True)  46 us
    dot_general x4, local copies, waits for them, and re-layouts, project_qkv(): jnp.dot(tokens_in, w_project, preferred_element_type=jnp.float32)  9.41 us
    all_to_all x1, starting transfers between devices, shards(): lax.all_to_all(local_keys, 'xy', split_axis=0, concat_axis=1, tiled=True)  5.78 us
    all_to_all x1, waiting for transfers between devices, shards(): lax.all_to_all(out_project(y_mix, full_out[1]), 'xy', split_axis=1, conca...  5.35 us
    all_to_all x1, waiting for transfers between devices, shards(): lax.all_to_all(local_keys, 'xy', split_axis=0, concat_axis=1, tiled=True)  5.24 us
    all_to_all x1, waiting for transfers between devices, shards(): lax.all_to_all(local_values, 'xy', split_axis=0, concat_axis=1, tiled=True)  5.21 us
    dot_general x3, matrix products, project_qkv(): jnp.dot(tokens_in, w_project, preferred_element_type=jnp.float32)  4.68 us
    unnamed x22, local copies, waits for them, and re-layouts  4.68 us
  transfers between devices with their start and end apart: 8, of which 7 were waited for; matrix products, arithmetic and copies ran while one was open for 25% of the time, Pallas kernels for 0%

commit v1 on v0

--- a/solution.py
+++ b/solution.py
@@ -5,6 +5,29 @@
 from jax.sharding import PartitionSpec as P
 
 EPSILON = 1e-06
+
+
+def in_blocks(value, dim, size):
+    lengths = value.shape
+    blocks = value.reshape(*lengths[:dim], size, lengths[dim] // size, *lengths[dim + 1 :])
+    return jnp.moveaxis(blocks, dim, 0)
+
+
+def laid_out(blocks, dim):
+    blocks = jnp.moveaxis(blocks, 0, dim)
+    shape = blocks.shape
+    return blocks.reshape(*shape[:dim], shape[dim] * shape[dim + 1], *shape[dim + 2 :])
+
+
+def exchange_in_pairs(x, axis, split_dim, concat_dim):
+    size, index = (lax.axis_size(axis), lax.axis_index(axis))
+    pieces = in_blocks(x, split_dim, size)
+    done = [pieces[index]]
+    for step in range(1, size):
+        sent = pieces[index ^ step]
+        done.append(lax.ppermute(sent, axis, [(i, i ^ step) for i in range(size)]))
+    pieces = jnp.stack(done)[index ^ jnp.arange(size)]
+    return laid_out(pieces, concat_dim)
 
 
 def rms_scale(vector_rows):
@@ -88,8 +111,8 @@
         values_along_y[:, :, None, :],
         score_scaling[1],
     )[:, :, 0, :]
-    second_direction_answer = lax.all_to_all(
-        out_project(y_mix, full_out[1]), "xy", split_axis=1, concat_axis=0, tiled=True
+    second_direction_answer = exchange_in_pairs(
+        out_project(y_mix, full_out[1]), "xy", 1, 0
     ).reshape(hidden_features.shape)
     pieces = project_qkv(
         lax.all_to_all(normed, "gz", split_axis=1, concat_axis=0, tiled=True),

time: 149 us -> 159 us (1.067)
  starting transfers between devices: 24.1 us -> 41.7 us
  waiting for transfers between devices: 69.6 us -> 62.6 us
  matrix products: 13.7 us -> 12 us
    ppermute x0 -> x15, starting transfers between devices: none -> 20.9 us  [exchange_in_pairs(): done.append(lax.ppermute(sent, axis, [(i, i ^ step) for i in range(size)]))]
    all_to_all x1 -> x0, waiting for transfers between devices: 5.35 us -> none  [shards(): lax.all_to_all(out_project(y_mix, full_out[1]), 'xy', split_axis=1, conca...]
    all_to_all x1, waiting for transfers between devices: 4.43 us -> 0.01 us  [shards(): lax.all_to_all(result_rows, 'gz', split_axis=0, concat_axis=1, tiled=True)]
    all_to_all x1 -> x0, starting transfers between devices: 3.64 us -> none  [shards(): lax.all_to_all(out_project(y_mix, full_out[1]), 'xy', split_axis=1, conca...]
    ppermute x0 -> x15, waiting for transfers between devices: none -> 2.51 us  [exchange_in_pairs(): done.append(lax.ppermute(sent, axis, [(i, i ^ step) for i in range(size)]))]
    all_to_all x1, waiting for transfers between devices: 5.24 us -> 7.1 us  [shards(): lax.all_to_all(local_keys, 'xy', split_axis=0, concat_axis=1, tiled=True)]
    unnamed x22 -> x37, local copies, waits for them, and re-layouts: 4.68 us -> 5.54 us
  transfers between devices with their start and end apart: 8 -> 22, of which waited for: 7 -> 7; matrix products, arithmetic and copies ran while one was open for 25% -> 23% of each run, Pallas kernels for 0% -> 0%
where the time goes in v1:
time: 159 us
  waiting for transfers between devices  62.6 us (39%)
  starting transfers between devices  41.7 us (26%)
  local copies, waits for them, and re-layouts  19.8 us (12%)
  between operations  14.7 us (9%)
  matrix products  12 us (8%)
  other arithmetic  7.85 us (5%)
    all_gather x1, waiting for transfers between devices, shards(): lax.all_gather(attention_input_matrices, 'xy', axis=1, tiled=True)  46 us
    ppermute x15, starting transfers between devices, exchange_in_pairs(): done.append(lax.ppermute(sent, axis, [(i, i ^ step) for i in range(size)]))  20.9 us
    dot_general x4, local copies, waits for them, and re-layouts, project_qkv(): jnp.dot(tokens_in, w_project, preferred_element_type=jnp.float32)  8.8 us
    all_to_all x1, waiting for transfers between devices, shards(): lax.all_to_all(local_keys, 'xy', split_axis=0, concat_axis=1, tiled=True)  7.1 us
    all_to_all x1, starting transfers between devices, shards(): lax.all_to_all(local_keys, 'xy', split_axis=0, concat_axis=1, tiled=True)  6.02 us
    unnamed x37, local copies, waits for them, and re-layouts  5.54 us
    dot_general x3, matrix products, project_qkv(): jnp.dot(tokens_in, w_project, preferred_element_type=jnp.float32)  5.28 us
    all_to_all x1, waiting for transfers between devices, shards(): lax.all_to_all(local_values, 'xy', split_axis=0, concat_axis=1, tiled=True)  4.64 us
  transfers between devices with their start and end apart: 22, of which 7 were waited for; matrix products, arithmetic and copies ran while one was open for 23% of the time, Pallas kernels for 0%

profile of v1, /device:TPU:0, one launch (start us, length us, event | category | flops | bytes accessed | tf_op | source)
XLA Modules:
  0.0 158.7 jit_solution(6821034297756731035)
XLA Ops:
  6.5 0.7 all-gather.3.cloned.1.call-update
  7.3 1.0 fusion.23
  8.3 1.0 fusion.25
  9.3 0.7 copy.529
  10.0 4.2 %all-to-all-start = ((bf16[8,16,1,512]{3,0,2,1:T(8,128)(2,1)}), bf16[8,16,1,512]{3,0,2,1:T(8,128)(2,1)S(1)}, u32[]{:S(2)}, u32[]{:S(2)}) async-start(bf16[8,16,1,512]{3,0,2,1:T(8,128)(2,1)} %copy.529), calls=%async_computation | async-start | bytes 262144 | tf_op jit(solution)/shard_map/all_to_all | solution.py:118
  14.3 0.7 all-gather.5.cloned.1.call-update
  15.1 1.3 multiply_bitcast_fusion.2
  17.1 0.8 and_reduce_fusion
  18.0 0.9 all-to-all-done
  18.8 0.7 copy.530
  19.5 46.0 %all-gather.3.cloned.1.call-done = bf16[3,512,1536]{2,1,0:T(8,128)(2,1)} async-done(((bf16[3,32,1536]{2,1,0:T(8,128)(2,1)}), bf16[3,512,1536]{2,1,0:T(8,128)(2,1)}) %all-gather.3.cloned.1.call-update) | async-done | bytes 4718608 | tf_op jit(solution)/shard_map/all_gather | solution.py:91
  65.5 3.9 %slice_bitcast_fusion.2 = (bf16[1536,512]{0,1:T(8,128)(2,1)S(1)}, bf16[1536,512]{0,1:T(8,128)(2,1)S(1)}, bf16[1536,512]{0,1:T(8,128)(2,1)}) fusion(bf16[3,512,1536]{2,1,0:T(8,128)(2,1)} %all-gather.3.cloned.1.call-done), kind=kLoop, calls=%fused_computation.6 | loop fusion | bytes 9437184 | tf_op jit(solution)/shard_map/dot_general | solution.py:40
  69.4 2.6 %copy.539 = bf16[1536,512]{1,0:T(8,128)(2,1)} copy(bf16[1536,512]{0,1:T(8,128)(2,1)} %get-tuple-element.13) | data formatting | bytes 3145728 | tf_op jit(solution)/shard_map/dot_general | solution.py:40
  72.0 2.0 %convolution_bitcast_fusion.2 = f32[128,1,3,8,64]{0,4,3,2,1:T(8,128)S(1)} fusion(bf16[128,512,1,1]{1,0,3,2:T(8,128)(2,1)S(1)} %bitcast.231, bf16[3,8,64,512]{3,2,1,0:T(8,128)(2,1)} %bitcast.230), kind=kOutput, calls=%fused_computation.9 | convolution fusion | flops 201326592 | bytes 2490368 | tf_op jit(solution)/shard_map/dot_general | solution.py:40
  74.0 0.9 copy-done
  75.6 1.3 reduce.26
  76.9 1.0 copy.638
  77.9 0.7 reshape.639
  78.6 3.5 %all-to-all-start.3 = ((bf16[16,2,2048]{2,1,0:T(2,128)(2,1)}), bf16[16,2,2048]{2,1,0:T(2,128)(2,1)S(1)}, u32[]{:S(2)}, u32[]{:S(2)}) async-start(bf16[16,2,2048]{2,1,0:T(2,128)(2,1)} %reshape.639), calls=%async_computation.3 | async-start | bytes 262144 | tf_op jit(solution)/shard_map/all_to_all | solution.py:104
  82.1 1.6 %copy.531 = bf16[1536,512]{1,0:T(8,128)(2,1)} copy(bf16[1536,512]{0,1:T(8,128)(2,1)S(1)} %get-tuple-element.11) | data formatting | bytes 3145728 | tf_op jit(solution)/shard_map/dot_general | solution.py:40
  83.7 0.7 copy.551
  84.4 2.4 %convolution_bitcast_fusion.1 = f32[16,8,1,3,8,64]{5,1,4,3,0,2:T(8,128)S(1)} fusion(bf16[16,8,512,1,1]{2,1,4,3,0:T(8,128)(2,1)} %bitcast.237, bf16[3,8,64,512,1]{3,2,1,0,4:T(8,128)(2,1)} %bitcast.229), kind=kOutput, calls=%fused_computation.8 | convolution fusion | flops 201326592 | bytes 2490368 | tf_op jit(solution)/shard_map/dot_general | solution.py:40
  87.6 0.8 fusion.61
  88.4 1.0 fusion.9
  89.4 0.9 convolution_bitcast_fusion
  90.7 1.0 slice.124
  91.8 0.6 reduce.25
  92.5 0.7 reshape.637
  93.9 0.7 reshape.641
  95.0 6.0 %all-to-all-start.4 = ((bf16[16,2,2048]{2,1,0:T(2,128)(2,1)}), bf16[16,2,2048]{2,1,0:T(2,128)(2,1)S(1)}, u32[]{:S(2)}, u32[]{:S(2)}) async-start(bf16[16,2,2048]{2,1,0:T(2,128)(2,1)} %reshape.637), calls=%async_computation.4 | async-start | bytes 262144 | tf_op jit(solution)/shard_map/all_to_all | solution.py:105
  101.0 0.8 fusion.55
  101.8 7.1 %all-to-all-done.4 = bf16[16,2,2048]{2,1,0:T(2,128)(2,1)S(1)} async-done(((bf16[16,2,2048]{2,1,0:T(2,128)(2,1)}), bf16[16,2,2048]{2,1,0:T(2,128)(2,1)S(1)}, u32[]{:S(2)}, u32[]{:S(2)}) %all-to-all-start.4) | async-done | bytes 131104 | tf_op jit(solution)/shard_map/all_to_all | solution.py:105
  108.9 3.5 %all-to-all-start.2 = ((bf16[16,2,2048]{2,1,0:T(2,128)(2,1)}), bf16[16,2,2048]{2,1,0:T(2,128)(2,1)S(1)}, u32[]{:S(2)}, u32[]{:S(2)}) async-start(bf16[16,2,2048]{2,1,0:T(2,128)(2,1)} %reshape.641), calls=%async_computation.2 | async-start | bytes 262144 | tf_op jit(solution)/shard_map/all_to_all | solution.py:106
  113.0 1.9 %fusion.12 = bf16[16,8,1,512]{3,1,2,0:T(8,128)(2,1)} fusion(bf16[16,8,512]{2,1,0:T(8,128)(2,1)S(1)} %reshape.600, bf16[3,512,512]{2,1,0:T(8,128)(2,1)} %all-gather.5.cloned.1.call-done), kind=kOutput, calls=%fused_computation.28 | convolution fusion | flops 67174400 | bytes 786432 | tf_op jit(solution)/shard_map/dot_general | solution.py:78
  115.6 4.6 %all-to-all-done.2 = bf16[16,2,2048]{2,1,0:T(2,128)(2,1)S(1)} async-done(((bf16[16,2,2048]{2,1,0:T(2,128)(2,1)}), bf16[16,2,2048]{2,1,0:T(2,128)(2,1)S(1)}, u32[]{:S(2)}, u32[]{:S(2)}) %all-to-all-start.2) | async-done | bytes 131104 | tf_op jit(solution)/shard_map/all_to_all | solution.py:106
  120.3 3.6 %all-to-all-start.1 = ((bf16[16,8,1,512]{3,1,2,0:T(8,128)(2,1)}), bf16[16,8,1,512]{3,1,2,0:T(8,128)(2,1)S(1)}, u32[]{:S(2)}, u32[]{:S(2)}) async-start(bf16[16,8,1,512]{3,1,2,0:T(8,128)(2,1)} %fusion.12), calls=%async_computation.1 | async-start | bytes 262144 | tf_op jit(solution)/shard_map/all_to_all | solution.py:131
  125.3 0.8 copy-done.3
  127.0 1.8 %collective-permute-start.2 = (bf16[8,1,512]{2,1,0:T(2,128)(2,1)S(1)}, bf16[8,1,512]{2,1,0:T(2,128)(2,1)S(1)}, u32[]{:S(2)}, u32[]{:S(2)}) collective-permute-start(bf16[8,1,512]{2,1,0:T(2,128)(2,1)S(1)} %get-tuple-element.30), channel_id=1, source_target_pairs={{0,6},{2,4},{4,2},{6,0},{8,14},{10,12},{12,10},{14,8},{16,22},{18,... | collective-permute-start | bytes 24584 | tf_op jit(solution)/shard_map/ppermute | solution.py:28
  128.7 1.7 %collective-permute-start.4 = (bf16[8,1,512]{2,1,0:T(2,128)(2,1)S(1)}, bf16[8,1,512]{2,1,0:T(2,128)(2,1)S(1)}, u32[]{:S(2)}, u32[]{:S(2)}) collective-permute-start(bf16[8,1,512]{2,1,0:T(2,128)(2,1)S(1)} %get-tuple-element.28), channel_id=1, source_target_pairs={{0,10},{2,8},{4,14},{6,12},{8,2},{10,0},{12,6},{14,4},{16,26},{18,... | collective-permute-start | bytes 24584 | tf_op jit(solution)/shard_map/ppermute | solution.py:28
  130.7 2.5 %collective-permute-start.6 = (bf16[8,1,512]{2,1,0:T(2,128)(2,1)S(1)}, bf16[8,1,512]{2,1,0:T(2,128)(2,1)S(1)}, u32[]{:S(2)}, u32[]{:S(2)}) collective-permute-start(bf16[8,1,512]{2,1,0:T(2,128)(2,1)S(1)} %get-tuple-element.26), channel_id=1, source_target_pairs={{0,14},{2,12},{4,10},{6,8},{8,6},{10,4},{12,2},{14,0},{16,30},{18,... | collective-permute-start | bytes 24584 | tf_op jit(solution)/shard_map/ppermute | solution.py:28
  133.6 2.4 %collective-permute-start.8 = (bf16[8,1,512]{2,1,0:T(2,128)(2,1)S(1)}, bf16[8,1,512]{2,1,0:T(2,128)(2,1)S(1)}, u32[]{:S(2)}, u32[]{:S(2)}) collective-permute-start(bf16[8,1,512]{2,1,0:T(2,128)(2,1)S(1)} %get-tuple-element.24), channel_id=1, source_target_pairs={{0,18},{2,16},{4,22},{6,20},{8,26},{10,24},{12,30},{14,28},{16,2},... | collective-permute-start | bytes 24584 | tf_op jit(solution)/shard_map/ppermute | solution.py:28
  136.3 3.3 %collective-permute-start.10 = (bf16[8,1,512]{2,1,0:T(2,128)(2,1)S(1)}, bf16[8,1,512]{2,1,0:T(2,128)(2,1)S(1)}, u32[]{:S(2)}, u32[]{:S(2)}) collective-permute-start(bf16[8,1,512]{2,1,0:T(2,128)(2,1)S(1)} %get-tuple-element.22), channel_id=1, source_target_pairs={{0,22},{2,20},{4,18},{6,16},{8,30},{10,28},{12,26},{14,24},{16,6},... | collective-permute-start | bytes 24584 | tf_op jit(solution)/shard_map/ppermute | solution.py:28
  139.7 0.7 collective-permute-start.11
  140.4 2.9 %collective-permute-start.12 = (bf16[8,1,512]{2,1,0:T(2,128)(2,1)S(1)}, bf16[8,1,512]{2,1,0:T(2,128)(2,1)S(1)}, u32[]{:S(2)}, u32[]{:S(2)}) collective-permute-start(bf16[8,1,512]{2,1,0:T(2,128)(2,1)S(1)} %get-tuple-element.20), channel_id=1, source_target_pairs={{0,26},{2,24},{4,30},{6,28},{8,18},{10,16},{12,22},{14,20},{16,10}... | collective-permute-start | bytes 24584 | tf_op jit(solution)/shard_map/ppermute | solution.py:28
  143.3 1.1 collective-permute-start.13
  144.4 3.5 %collective-permute-start.14 = (bf16[8,1,512]{2,1,0:T(2,128)(2,1)S(1)}, bf16[8,1,512]{2,1,0:T(2,128)(2,1)S(1)}, u32[]{:S(2)}, u32[]{:S(2)}) collective-permute-start(bf16[8,1,512]{2,1,0:T(2,128)(2,1)S(1)} %get-tuple-element.18), channel_id=1, source_target_pairs={{0,30},{2,28},{4,26},{6,24},{8,22},{10,20},{12,18},{14,16},{16,14}... | collective-permute-start | bytes 24584 | tf_op jit(solution)/shard_map/ppermute | solution.py:28
  148.0 1.8 %collective-permute-done.13 = bf16[8,1,512]{2,1,0:T(2,128)(2,1)S(1)} collective-permute-done((bf16[8,1,512]{2,1,0:T(2,128)(2,1)S(1)}, bf16[8,1,512]{2,1,0:T(2,128)(2,1)S(1)}, u32[]{:S(2)}, u32[]{:S(2)}) %collective-permute-start.13) | collective-permute-done | bytes 8224 | tf_op jit(solution)/shard_map/ppermute | solution.py:28
  150.9 0.9 fusion.18
  (91 shorter events, 8.6 us)
Async XLA Ops:
  6.5 59.0 %all-gather.3.cloned.1.call-start = ((), (), s32[]{:S(2)}) async-start(), calls=%async_computation.5 | async-start | bytes 5013504 | tf_op jit(solution)/shard_map/all_gather | solution.py:91
  10.0 8.8 %all-to-all-start = ((bf16[8,16,1,512]{3,0,2,1:T(8,128)(2,1)}), bf16[8,16,1,512]{3,0,2,1:T(8,128)(2,1)S(1)}, u32[]{:S(2)}, u32[]{:S(2)}) async-start(bf16[8,16,1,512]{3,0,2,1:T(8,128)(2,1)} %copy.529), calls=%async_computation | async-start | bytes 262144 | tf_op jit(solution)/shard_map/all_to_all | solution.py:118
  14.3 98.7 %all-gather.5.cloned.1.call-start = ((), (), s32[]{:S(2)}) async-start(), calls=%async_computation.6 | async-start | bytes 1671168 | tf_op jit(solution)/shard_map/all_gather | solution.py:92
  74.0 0.9 copy-start
  78.6 16.4 %all-to-all-start.3 = ((bf16[16,2,2048]{2,1,0:T(2,128)(2,1)}), bf16[16,2,2048]{2,1,0:T(2,128)(2,1)S(1)}, u32[]{:S(2)}, u32[]{:S(2)}) async-start(bf16[16,2,2048]{2,1,0:T(2,128)(2,1)} %reshape.639), calls=%async_computation.3 | async-start | bytes 262144 | tf_op jit(solution)/shard_map/all_to_all | solution.py:104
  86.8 0.8 copy-start.4
  90.3 4.3 %copy-start.2 = (bf16[1,16,8,8,64]{4,1,3,2,0:T(8,128)(2,1)S(1)}, bf16[1,16,8,8,64]{4,1,3,2,0:T(8,128)(2,1)}, u32[]{:S(2)}) copy-start(bf16[1,16,8,8,64]{4,1,3,2,0:T(8,128)(2,1)} %fusion.9) | copy-start | bytes 393220
  95.0 13.9 %all-to-all-start.4 = ((bf16[16,2,2048]{2,1,0:T(2,128)(2,1)}), bf16[16,2,2048]{2,1,0:T(2,128)(2,1)S(1)}, u32[]{:S(2)}, u32[]{:S(2)}) async-start(bf16[16,2,2048]{2,1,0:T(2,128)(2,1)} %reshape.637), calls=%async_computation.4 | async-start | bytes 262144 | tf_op jit(solution)/shard_map/all_to_all | solution.py:105
  108.9 11.4 %all-to-all-start.2 = ((bf16[16,2,2048]{2,1,0:T(2,128)(2,1)}), bf16[16,2,2048]{2,1,0:T(2,128)(2,1)S(1)}, u32[]{:S(2)}, u32[]{:S(2)}) async-start(bf16[16,2,2048]{2,1,0:T(2,128)(2,1)} %reshape.641), calls=%async_computation.2 | async-start | bytes 262144 | tf_op jit(solution)/shard_map/all_to_all | solution.py:106
  120.3 30.6 %all-to-all-start.1 = ((bf16[16,8,1,512]{3,1,2,0:T(8,128)(2,1)}), bf16[16,8,1,512]{3,1,2,0:T(8,128)(2,1)S(1)}, u32[]{:S(2)}, u32[]{:S(2)}) async-start(bf16[16,8,1,512]{3,1,2,0:T(8,128)(2,1)} %fusion.12), calls=%async_computation.1 | async-start | bytes 262144 | tf_op jit(solution)/shard_map/all_to_all | solution.py:131
  124.7 1.4 copy-start.3
  125.0 25.9 %copy-start.1 = (bf16[8,16,1,512]{3,1,2,0:T(8,128)(2,1)S(1)}, bf16[8,16,1,512]{3,1,2,0:T(8,128)(2,1)}, u32[]{:S(2)}) copy-start(bf16[8,16,1,512]{3,1,2,0:T(8,128)(2,1)} %param.7) | copy-start | bytes 393220
  126.8 3.7 %collective-permute-start = (bf16[8,1,512]{2,1,0:T(2,128)(2,1)S(1)}, bf16[8,1,512]{2,1,0:T(2,128)(2,1)S(1)}, u32[]{:S(2)}, u32[]{:S(2)}) collective-permute-start(bf16[8,1,512]{2,1,0:T(2,128)(2,1)S(1)} %get-tuple-element.32), channel_id=1, source_target_pairs={{0,2},{2,0},{4,6},{6,4},{8,10},{10,8},{12,14},{14,12},{16,18},{18,... | collective-permute-start | bytes 24584 | tf_op jit(solution)/shard_map/ppermute | solution.py:28
  126.9 3.8 %collective-permute-start.1 = (bf16[8,1,512]{2,1,0:T(2,128)(2,1)S(1)}, bf16[8,1,512]{2,1,0:T(2,128)(2,1)S(1)}, u32[]{:S(2)}, u32[]{:S(2)}) collective-permute-start(bf16[8,1,512]{2,1,0:T(2,128)(2,1)S(1)} %get-tuple-element.31), channel_id=1, source_target_pairs={{0,4},{2,6},{4,0},{6,2},{8,12},{10,14},{12,8},{14,10},{16,20},{18,... | collective-permute-start | bytes 24584 | tf_op jit(solution)/shard_map/ppermute | solution.py:28
  127.0 6.2 %collective-permute-start.2 = (bf16[8,1,512]{2,1,0:T(2,128)(2,1)S(1)}, bf16[8,1,512]{2,1,0:T(2,128)(2,1)S(1)}, u32[]{:S(2)}, u32[]{:S(2)}) collective-permute-start(bf16[8,1,512]{2,1,0:T(2,128)(2,1)S(1)} %get-tuple-element.30), channel_id=1, source_target_pairs={{0,6},{2,4},{4,2},{6,0},{8,14},{10,12},{12,10},{14,8},{16,22},{18,... | collective-permute-start | bytes 24584 | tf_op jit(solution)/shard_map/ppermute | solution.py:28
  128.7 4.9 %collective-permute-start.3 = (bf16[8,1,512]{2,1,0:T(2,128)(2,1)S(1)}, bf16[8,1,512]{2,1,0:T(2,128)(2,1)S(1)}, u32[]{:S(2)}, u32[]{:S(2)}) collective-permute-start(bf16[8,1,512]{2,1,0:T(2,128)(2,1)S(1)} %get-tuple-element.29), channel_id=1, source_target_pairs={{0,8},{2,10},{4,12},{6,14},{8,0},{10,2},{12,4},{14,6},{16,24},{18,... | collective-permute-start | bytes 24584 | tf_op jit(solution)/shard_map/ppermute | solution.py:28
  128.7 7.2 %collective-permute-start.4 = (bf16[8,1,512]{2,1,0:T(2,128)(2,1)S(1)}, bf16[8,1,512]{2,1,0:T(2,128)(2,1)S(1)}, u32[]{:S(2)}, u32[]{:S(2)}) collective-permute-start(bf16[8,1,512]{2,1,0:T(2,128)(2,1)S(1)} %get-tuple-element.28), channel_id=1, source_target_pairs={{0,10},{2,8},{4,14},{6,12},{8,2},{10,0},{12,6},{14,4},{16,26},{18,... | collective-permute-start | bytes 24584 | tf_op jit(solution)/shard_map/ppermute | solution.py:28
  130.5 5.9 %collective-permute-start.5 = (bf16[8,1,512]{2,1,0:T(2,128)(2,1)S(1)}, bf16[8,1,512]{2,1,0:T(2,128)(2,1)S(1)}, u32[]{:S(2)}, u32[]{:S(2)}) collective-permute-start(bf16[8,1,512]{2,1,0:T(2,128)(2,1)S(1)} %get-tuple-element.27), channel_id=1, source_target_pairs={{0,12},{2,14},{4,8},{6,10},{8,4},{10,6},{12,0},{14,2},{16,28},{18,... | collective-permute-start | bytes 24584 | tf_op jit(solution)/shard_map/ppermute | solution.py:28
  130.7 9.0 %collective-permute-start.6 = (bf16[8,1,512]{2,1,0:T(2,128)(2,1)S(1)}, bf16[8,1,512]{2,1,0:T(2,128)(2,1)S(1)}, u32[]{:S(2)}, u32[]{:S(2)}) collective-permute-start(bf16[8,1,512]{2,1,0:T(2,128)(2,1)S(1)} %get-tuple-element.26), channel_id=1, source_target_pairs={{0,14},{2,12},{4,10},{6,8},{8,6},{10,4},{12,2},{14,0},{16,30},{18,... | collective-permute-start | bytes 24584 | tf_op jit(solution)/shard_map/ppermute | solution.py:28
  133.2 7.2 %collective-permute-start.7 = (bf16[8,1,512]{2,1,0:T(2,128)(2,1)S(1)}, bf16[8,1,512]{2,1,0:T(2,128)(2,1)S(1)}, u32[]{:S(2)}, u32[]{:S(2)}) collective-permute-start(bf16[8,1,512]{2,1,0:T(2,128)(2,1)S(1)} %get-tuple-element.25), channel_id=1, source_target_pairs={{0,16},{2,18},{4,20},{6,22},{8,24},{10,26},{12,28},{14,30},{16,0},... | collective-permute-start | bytes 24584 | tf_op jit(solution)/shard_map/ppermute | solution.py:28
  133.6 9.7 %collective-permute-start.8 = (bf16[8,1,512]{2,1,0:T(2,128)(2,1)S(1)}, bf16[8,1,512]{2,1,0:T(2,128)(2,1)S(1)}, u32[]{:S(2)}, u32[]{:S(2)}) collective-permute-start(bf16[8,1,512]{2,1,0:T(2,128)(2,1)S(1)} %get-tuple-element.24), channel_id=1, source_target_pairs={{0,18},{2,16},{4,22},{6,20},{8,26},{10,24},{12,30},{14,28},{16,2},... | collective-permute-start | bytes 24584 | tf_op jit(solution)/shard_map/ppermute | solution.py:28
  136.0 8.5 %collective-permute-start.9 = (bf16[8,1,512]{2,1,0:T(2,128)(2,1)S(1)}, bf16[8,1,512]{2,1,0:T(2,128)(2,1)S(1)}, u32[]{:S(2)}, u32[]{:S(2)}) collective-permute-start(bf16[8,1,512]{2,1,0:T(2,128)(2,1)S(1)} %get-tuple-element.23), channel_id=1, source_target_pairs={{0,20},{2,22},{4,16},{6,18},{8,28},{10,30},{12,24},{14,26},{16,4},... | collective-permute-start | bytes 24584 | tf_op jit(solution)/shard_map/ppermute | solution.py:28
  136.3 11.6 %collective-permute-start.10 = (bf16[8,1,512]{2,1,0:T(2,128)(2,1)S(1)}, bf16[8,1,512]{2,1,0:T(2,128)(2,1)S(1)}, u32[]{:S(2)}, u32[]{:S(2)}) collective-permute-start(bf16[8,1,512]{2,1,0:T(2,128)(2,1)S(1)} %get-tuple-element.22), channel_id=1, source_target_pairs={{0,22},{2,20},{4,18},{6,16},{8,30},{10,28},{12,26},{14,24},{16,6},... | collective-permute-start | bytes 24584 | tf_op jit(solution)/shard_map/ppermute | solution.py:28
  139.7 8.3 %collective-permute-start.11 = (bf16[8,1,512]{2,1,0:T(2,128)(2,1)S(1)}, bf16[8,1,512]{2,1,0:T(2,128)(2,1)S(1)}, u32[]{:S(2)}, u32[]{:S(2)}) collective-permute-start(bf16[8,1,512]{2,1,0:T(2,128)(2,1)S(1)} %get-tuple-element.21), channel_id=1, source_target_pairs={{0,24},{2,26},{4,28},{6,30},{8,16},{10,18},{12,20},{14,22},{16,8},... | collective-permute-start | bytes 24584 | tf_op jit(solution)/shard_map/ppermute | solution.py:28
  140.4 7.6 %collective-permute-start.12 = (bf16[8,1,512]{2,1,0:T(2,128)(2,1)S(1)}, bf16[8,1,512]{2,1,0:T(2,128)(2,1)S(1)}, u32[]{:S(2)}, u32[]{:S(2)}) collective-permute-start(bf16[8,1,512]{2,1,0:T(2,128)(2,1)S(1)} %get-tuple-element.20), channel_id=1, source_target_pairs={{0,26},{2,24},{4,30},{6,28},{8,18},{10,16},{12,22},{14,20},{16,10}... | collective-permute-start | bytes 24584 | tf_op jit(solution)/shard_map/ppermute | solution.py:28
  143.3 6.5 %collective-permute-start.13 = (bf16[8,1,512]{2,1,0:T(2,128)(2,1)S(1)}, bf16[8,1,512]{2,1,0:T(2,128)(2,1)S(1)}, u32[]{:S(2)}, u32[]{:S(2)}) collective-permute-start(bf16[8,1,512]{2,1,0:T(2,128)(2,1)S(1)} %get-tuple-element.19), channel_id=1, source_target_pairs={{0,28},{2,30},{4,24},{6,26},{8,20},{10,22},{12,16},{14,18},{16,12}... | collective-permute-start | bytes 24584 | tf_op jit(solution)/shard_map/ppermute | solution.py:28
  144.4 5.9 %collective-permute-start.14 = (bf16[8,1,512]{2,1,0:T(2,128)(2,1)S(1)}, bf16[8,1,512]{2,1,0:T(2,128)(2,1)S(1)}, u32[]{:S(2)}, u32[]{:S(2)}) collective-permute-start(bf16[8,1,512]{2,1,0:T(2,128)(2,1)S(1)} %get-tuple-element.18), channel_id=1, source_target_pairs={{0,30},{2,28},{4,26},{6,24},{8,22},{10,20},{12,18},{14,16},{16,14}... | collective-permute-start | bytes 24584 | tf_op jit(solution)/shard_map/ppermute | solution.py:28
Sparse Core Ops, SparseCore 0:
  9.6 55.8 all-gather.2
  67.7 39.2 all-gather.4
